TPU v7x, 512 devices: a whole 4x4x16 slice. The times are simulated.
512 devices in a mesh: expert: 128 (over z, y_hi, x), half: 4 (over y_lo, core).
Axes of the slice: x: 4, y: 4 (y_hi: 2, y_lo: 2; y = y_hi * 2 + y_lo), z: 16, core: 2. Of those that a mesh axis runs over, the one named last changes fastest.
Arguments:
- tokens: bfloat16 [131072, 1024], P(('expert', 'half')), may hold values from -6 to 6
- router: bfloat16 [1024, 256], replicated, may hold values from -1 to 1
- w_in: bfloat16 [128, 1024, 3072], P('expert', None, 'half'), may hold values from -0.1875 to 0.1875
- w_out: bfloat16 [128, 3072, 1024], P('expert', 'half'), may hold values from -0.109375 to 0.109375
Outputs:
- mixed: bfloat16 [131072, 1024], P(('expert', 'half'))
All inputs are finite; a program needn't handle non-finite values.
Results may differ from a plain program's by a relative error of at most 0.018.
Values may be sent and summed in bfloat16 or wider, within the bound.
No kernel may reach another device: no remote copies, remote signals or barrier semaphores. Data moves between devices by JAX's collectives and lax.ppermute only.
A program may use at most 64 MiB of HBM per device.

v0:
```python
import jax
import jax.numpy as jnp
from jax import lax
from jax.sharding import PartitionSpec as P

SLOTS = 2
PATCHES = 256


def from_everyone(value, axis):
    length = lax.axis_size(axis)
    return lax.all_to_all(
        jnp.broadcast_to(value[None], (length, *value.shape)), axis, 0, 0, tiled=True
    )


def in_order(parts, dim):
    parts = jnp.moveaxis(parts, 0, dim)
    dims = parts.shape
    return parts.reshape(*dims[:dim], dims[dim] * dims[dim + 1], *dims[dim + 2 :])


def gathered_copies(value, axis, dim):
    parts = from_everyone(value, axis)
    return in_order(parts, dim)


def cut_along(value, dim, length):
    before, after = (value.shape[:dim], value.shape[dim + 1 :])
    return jnp.moveaxis(value.reshape(*before, length, -1, *after), dim, 0)


def summed_on_arrival(value, axis, dim):
    parts = cut_along(value, dim, lax.axis_size(axis))
    arrived = lax.all_to_all(parts, axis, split_axis=0, concat_axis=0, tiled=True)
    return arrived.astype(jnp.float32).sum(axis=0)


def expert_quarter(rows, first, second):
    hidden = jax.nn.gelu(
        jnp.einsum("erd,edf->erf", rows, first, preferred_element_type=jnp.float32)
    ).astype(jnp.bfloat16)
    return jnp.einsum("erf,efd->erd", hidden, second, preferred_element_type=jnp.float32)


def on_device(tokens, router, w_in, w_out):
    width = tokens.shape[1]
    images = tokens.shape[0] // PATCHES
    experts_all = router.shape[1] // SLOTS
    picture = tokens.reshape(images, PATCHES, width)
    logits = jnp.einsum("imd,dc->imc", picture, router, preferred_element_type=jnp.float32)
    dispatch = jax.nn.softmax(logits, axis=1).astype(jnp.bfloat16)
    combine = jax.nn.softmax(logits, axis=2).astype(jnp.bfloat16)
    slot_input = jnp.einsum(
        "imc,imd->icd", dispatch, picture, preferred_element_type=jnp.float32
    ).astype(jnp.bfloat16)
    outgoing = slot_input.reshape(images, experts_all, SLOTS, width)
    arrived = lax.all_to_all(outgoing, "expert", split_axis=1, concat_axis=0, tiled=True)
    local_experts = arrived.shape[1]
    slot_rows_local = jnp.transpose(arrived, (1, 0, 2, 3)).reshape(local_experts, -1, width)
    terms = expert_quarter(gathered_copies(slot_rows_local, "half", 1), w_in, w_out)
    result = summed_on_arrival(terms.astype(jnp.bfloat16), "half", 1)
    back = jnp.transpose(
        result.astype(jnp.bfloat16).reshape(local_experts, -1, SLOTS, width), (1, 0, 2, 3)
    )
    returned = lax.all_to_all(back, "expert", split_axis=0, concat_axis=1, tiled=True)
    slot_output = returned.reshape(images, experts_all * SLOTS, width)
    mixed = jnp.einsum(
        "imc,icd->imd", combine, slot_output, preferred_element_type=jnp.float32
    ).astype(jnp.bfloat16)
    return mixed.reshape(-1, width)


def solution(mesh):
    return jax.shard_map(
        on_device,
        mesh=mesh,
        in_specs=(
            P(("expert", "half"), None),
            P(),
            P("expert", None, "half"),
            P("expert", "half", None),
        ),
        out_specs=P(("expert", "half"), None),
        check_vma=False,
    )
```

profile of v0, /device:TPU:32, one launch (start us, length us, event | category | flops | bytes accessed | tf_op | source)
XLA Modules:
  0.0 171.6 jit_solution(13309101023838386148)
XLA Ops:
  0.0 0.0 copy-start
  0.0 1.7 fusion.30
  1.7 0.2 fusion.20
  1.9 1.4 convolution_convert_fusion.2
  3.3 0.2 reshape.92
  3.5 56.3 %all_to_all.28 = bf16[1,128,2,1024]{3,2,0,1:T(2,128)(2,1)S(1)} all-to-all(bf16[1,128,2,1024]{3,2,0,1:T(2,128)(2,1)S(1)} %bitcast.24), channel_id=1, replica_groups=mesh['expert'=128,'half'=4] {'expert'}, dimensions={1} | all-to-all | bytes 1048576 | tf_op jit(solution)/shard_map/all_to_all | solution.py:58
  59.8 0.2 broadcast_in_dim.4
  60.0 0.3 broadcast_in_dim.5
  60.3 0.0 copy-start.1
  60.3 29.0 %all_to_all.29 = bf16[4,1,256,1024]{3,2,1,0:T(8,128)(2,1)} all-to-all(bf16[4,1,256,1024]{3,2,1,0:T(8,128)(2,1)S(1)} %broadcast_in_dim.5), channel_id=1, replica_groups=mesh['expert'=128,'half'=4] {'half'}, dimensions={0} | all-to-all | bytes 4194304 | tf_op jit(solution)/shard_map/all_to_all | solution.py:12
  89.3 0.0 copy-done
  89.3 0.0 copy-done.1
  89.3 7.4 %convolution_convert_fusion = bf16[1024,1024]{1,0:T(8,128)(2,1)} fusion(bf16[1,768,1024]{2,1,0:T(8,128)(2,1)S(1)} %copy-done, bf16[1024,1024]{1,0:T(8,128)(2,1)} %bitcast.22, bf16[1,1024,768]{2,1,0:T(8,128)(2,1)S(1)} %copy-done.1), kind=kOutput, calls=%fused_computation.9 | convolution fusion | flops 3229351936 | bytes 7340032 | tf_op jit(solution)/shard_map/erf,efd->erd/dot_general | solution.py:43
  96.8 30.1 %all_to_all.30 = bf16[4,1,256,1024]{3,2,1,0:T(8,128)(2,1)} all-to-all(bf16[4,1,256,1024]{3,2,1,0:T(8,128)(2,1)} %bitcast.23), channel_id=1, replica_groups=mesh['expert'=128,'half'=4] {'half'}, dimensions={0} | all-to-all | bytes 4194304 | tf_op jit(solution)/shard_map/all_to_all | solution.py:35
  126.9 2.0 %reduce_sum.32 = bf16[256,1024]{1,0:T(8,128)(2,1)S(1)} reduce(bf16[4,1,256,1024]{3,2,1,0:T(8,128)(2,1)} %all_to_all.30, bf16[]{:T(256)} %constant.14.clone.1), dimensions={0,1}, to_apply=%region_4.0 | reduce | flops 786432 | bytes 2621442 | tf_op jit(solution)/shard_map/reduce_sum | solution.py:36
  128.9 0.2 transpose_reshape.7
  129.1 41.1 %all_to_all.31 = bf16[128,1,2,1024]{3,2,1,0:T(2,128)(2,1)S(1)} all-to-all(bf16[128,1,2,1024]{3,2,1,0:T(2,128)(2,1)S(1)} %transpose_reshape.7), channel_id=1, replica_groups=mesh['expert'=128,'half'=4] {'expert'}, dimensions={0} | all-to-all | bytes 1048576 | tf_op jit(solution)/shard_map/all_to_all | solution.py:66
  170.3 0.2 reshape.96
  170.5 1.2 convolution_convert_fusion.1
Async XLA Ops:
  0.0 89.3 %copy-start = (bf16[1,768,1024]{2,1,0:T(8,128)(2,1)S(1)}, bf16[1,768,1024]{2,1,0:T(8,128)(2,1)}, u32[]{:S(2)}) copy-start(bf16[1,768,1024]{2,1,0:T(8,128)(2,1)} %param.7) | copy-start | bytes 4718596
  60.3 29.1 %copy-start.1 = (bf16[1,1024,768]{2,1,0:T(8,128)(2,1)S(1)}, bf16[1,1024,768]{2,1,0:T(8,128)(2,1)}, u32[]{:S(2)}) copy-start(bf16[1,1024,768]{2,1,0:T(8,128)(2,1)} %param.6) | copy-start | bytes 4718596
where the time goes:
time: 172 us
  blocking collectives  157 us (91%)
  matrix products  11.7 us (7%)
  other arithmetic  2.22 us (1%)
    all_to_all x1, blocking collectives, on_device(): lax.all_to_all(outgoing, 'expert', split_axis=1, concat_axis=0, tiled=True)  56.3 us
    all_to_all x1, blocking collectives, on_device(): lax.all_to_all(back, 'expert', split_axis=0, concat_axis=1, tiled=True)  41.1 us
    all_to_all x1, blocking collectives, summed_on_arrival(): lax.all_to_all(parts, axis, split_axis=0, concat_axis=0, tiled=True)  30.1 us
    all_to_all x1, blocking collectives, from_everyone(): lax.all_to_all(jnp.broadcast_to(value[None], (length, *value.shape)), axi...  29 us
    dot_general x1, matrix products, expert_quarter(): jnp.einsum('erf,efd->erd', hidden, second, preferred_element_type=jnp.flo...  7.43 us

commit v1 on v0

--- a/solution.py
+++ b/solution.py
@@ -55,7 +55,12 @@
         "imc,imd->icd", dispatch, picture, preferred_element_type=jnp.float32
     ).astype(jnp.bfloat16)
     outgoing = slot_input.reshape(images, experts_all, SLOTS, width)
-    arrived = lax.all_to_all(outgoing, "expert", split_axis=1, concat_axis=0, tiled=True)
+    arrived = jnp.concatenate(
+        lax.all_to_all(
+            jnp.stack(jnp.split(outgoing, lax.axis_size("expert"), axis=1)), "expert", 0, 0
+        ),
+        axis=0,
+    )
     local_experts = arrived.shape[1]
     slot_rows_local = jnp.transpose(arrived, (1, 0, 2, 3)).reshape(local_experts, -1, width)
     terms = expert_quarter(gathered_copies(slot_rows_local, "half", 1), w_in, w_out)

time: 172 us -> 174 us (1.012)
  no operation moved by 1% of the time
where the time goes in v1:
time: 174 us
  blocking collectives  156 us (90%)
  matrix products  12.1 us (7%)
  local copies, waits for them, and re-layouts  2.67 us (2%)
  other arithmetic  2.22 us (1%)
    all_to_all x1, blocking collectives, on_device(): lax.all_to_all(jnp.stack(jnp.split(outgoing, lax.axis_size('expert'), axi...  56.3 us
    all_to_all x1, blocking collectives, on_device(): lax.all_to_all(back, 'expert', split_axis=0, concat_axis=1, tiled=True)  41.2 us
    all_to_all x1, blocking collectives, summed_on_arrival(): lax.all_to_all(parts, axis, split_axis=0, concat_axis=0, tiled=True)  30.1 us
    all_to_all x1, blocking collectives, from_everyone(): lax.all_to_all(jnp.broadcast_to(value[None], (length, *value.shape)), axi...  28.9 us
    dot_general x1, matrix products, expert_quarter(): jnp.einsum('erf,efd->erd', hidden, second, preferred_element_type=jnp.flo...  7.86 us

profile of v1, /device:TPU:32, one launch (start us, length us, event | category | flops | bytes accessed | tf_op | source)
XLA Modules:
  0.0 173.9 jit_solution(11573361656570206778)
XLA Ops:
  0.0 0.0 copy-start
  0.0 1.7 fusion.30
  1.7 0.2 fusion.20
  1.9 1.4 convolution_convert_fusion.2
  3.3 0.2 reshape.88
  5.5 56.3 %all_to_all.24 = bf16[128,1,1,2,1024]{4,3,2,1,0:T(2,128)(2,1)S(1)} all-to-all(bf16[128,1,1,2,1024]{4,3,2,1,0:T(2,128)(2,1)S(1)} %constant_dynamic-update-slice_fusion), channel_id=1, replica_groups=mesh['expert'=128,'half'=4] {'expert'}, dimensions={0} | all-to-all | bytes 1048576 | tf_op jit(solution)/shard_map/all_to_all | solution.py:59
  61.8 0.2 broadcast_in_dim.4
  62.0 0.3 broadcast_in_dim.5
  62.3 28.9 %all_to_all.25 = bf16[4,1,256,1024]{3,2,1,0:T(8,128)(2,1)} all-to-all(bf16[4,1,256,1024]{3,2,1,0:T(8,128)(2,1)S(1)} %broadcast_in_dim.5), channel_id=1, replica_groups=mesh['expert'=128,'half'=4] {'half'}, dimensions={0} | all-to-all | bytes 4194304 | tf_op jit(solution)/shard_map/all_to_all | solution.py:12
  91.2 0.0 copy-done
  91.2 7.9 %convolution_convert_fusion = bf16[1024,1024]{1,0:T(8,128)(2,1)} fusion(bf16[1,768,1024]{2,1,0:T(8,128)(2,1)S(1)} %copy-done, bf16[1024,1024]{1,0:T(8,128)(2,1)} %bitcast.531, bf16[1,1024,768]{2,1,0:T(8,128)(2,1)} %param.6), kind=kOutput, calls=%fused_computation.9 | convolution fusion | flops 3229351936 | bytes 7340032 | tf_op jit(solution)/shard_map/erf,efd->erd/dot_general | solution.py:43
  99.0 30.1 %all_to_all.26 = bf16[4,1,256,1024]{3,2,1,0:T(8,128)(2,1)} all-to-all(bf16[4,1,256,1024]{3,2,1,0:T(8,128)(2,1)} %bitcast.532), channel_id=1, replica_groups=mesh['expert'=128,'half'=4] {'half'}, dimensions={0} | all-to-all | bytes 4194304 | tf_op jit(solution)/shard_map/all_to_all | solution.py:35
  129.2 2.0 %reduce_sum.32 = bf16[256,1024]{1,0:T(8,128)(2,1)S(1)} reduce(bf16[4,1,256,1024]{3,2,1,0:T(8,128)(2,1)} %all_to_all.26, bf16[]{:T(256)} %constant.14.clone.1), dimensions={0,1}, to_apply=%region_4.0 | reduce | flops 786432 | bytes 2621442 | tf_op jit(solution)/shard_map/reduce_sum | solution.py:36
  131.2 0.2 transpose_reshape.7
  131.4 41.2 %all_to_all.27 = bf16[128,1,2,1024]{3,2,1,0:T(2,128)(2,1)S(1)} all-to-all(bf16[128,1,2,1024]{3,2,1,0:T(2,128)(2,1)S(1)} %transpose_reshape.7), channel_id=1, replica_groups=mesh['expert'=128,'half'=4] {'expert'}, dimensions={0} | all-to-all | bytes 1048576 | tf_op jit(solution)/shard_map/all_to_all | solution.py:71
  172.5 0.2 reshape.92
  172.7 1.2 convolution_convert_fusion.1
  (128 shorter events, 1.6 us)
Async XLA Ops:
  0.0 91.2 %copy-start = (bf16[1,768,1024]{2,1,0:T(8,128)(2,1)S(1)}, bf16[1,768,1024]{2,1,0:T(8,128)(2,1)}, u32[]{:S(2)}) copy-start(bf16[1,768,1024]{2,1,0:T(8,128)(2,1)} %param.7) | copy-start | bytes 4718596
